TPU v7x, 32 devices: a whole 2x2x4 slice. The times are simulated.
32 devices in a mesh: rep: 2 (over x), node: 2 (over core), local: 8 (over z, y).
Axes of the slice: x: 2, y: 2, z: 4, core: 2. Of those that a mesh axis runs over, the one named last changes fastest.
Arguments:
- tokens: bfloat16 [1024, 3584], P(('rep', 'node', 'local')), parts along dimension 0, may hold values from -6 to 6
- expert_ids: int32 [1024, 8], P(('rep', 'node', 'local')), parts along dimension 0, may hold values from 0 to 15, all different within a row; in each aligned block of 32 rows (0 to 31, 32 to 63, ...) at most 32 rows name the same one
- route_weights: bfloat16 [1024, 8], P(('rep', 'node', 'local')), parts along dimension 0, may hold values from 0.099609375 to 1
- w_up: bfloat16 [16, 3584, 1024], P(('node', 'local')), may hold values from -0.09375 to 0.09375
- w_down: bfloat16 [16, 1024, 3584], P(('node', 'local')), may hold values from -0.1875 to 0.1875
Outputs:
- mixed: bfloat16 [1024, 3584], P(('rep', 'node', 'local')), parts along dimension 0
There are 2 independent parts, one for each index of `rep`. A program takes and returns all parts, laid end to end along the dimension named above; an argument that names none is the same for every part. Nothing has to cross between parts.
Inputs may be any that keep to these rules, and one draw needn't show every extreme that they name: `expert_ids`: the 8 experts of a token differ; in each aligned block of 32 rows (the rows of one device) no expert is named by more than 32 rows.
All inputs are finite; a program needn't handle non-finite values.
Results may differ from a plain program's by a relative error of at most 0.0058.
Values may be sent and summed in bfloat16 or wider, within the bound.
A program may use at most 64 MiB of HBM per device.

v0:
```python
import functools
import jax
import jax.numpy as jnp
from jax import lax
from jax.experimental import pallas as pl
from jax.experimental.pallas import tpu as pltpu
from jax.sharding import PartitionSpec as P

MESH = pl.DeviceIdType.MESH
LANES = 128
LAG_A, LAG_B, LAG_D, LAG_F, LAG_G, LAG_R = 1, 4, 5, 1, 4, 7
AHEAD = 3


def moe_kernel(sizes, x_hbm, ids_ref, weights_ref, up_hbm, down_hbm, out_ref,
               xg, wg, up, down, acc, hid, wcol,
               psend, pown, precv, ysend, yown, yrecv, zsend, zown, zrecv, rin,
               own_sem, up_sem, down_sem,
               gz_s, gz_r, gr_s, go_s, go_r, gy_s, gy_r, gp_s, gp_r,
               rp_s, rp_r, ro_s, ro_r, ry_s, ry_r, rz_s, rz_r, rr_s, rr_r):
    rows, major, chunks, width = sizes
    core = lax.axis_index("node")
    local = lax.axis_index("local")
    z, y = local // 2, lax.rem(local, 2)
    last = major - 1
    low, high = z == 0, z == last
    inner = (z == 1) | (z == last - 1)
    col_rows = major * rows
    half = 2 * col_rows

    def z_plus(d):
        return lax.rem(z + d, major)

    def near(zz):
        return {"local": zz * 2 + y}

    at_y = {"local": z * 2 + (1 - y)}
    at_p = {"node": 1 - core}

    barrier = pltpu.get_barrier_semaphore()
    peers = [near(z_plus(d)) for d in range(1, major)] + [at_y, at_p]
    for peer in peers:
        pl.semaphore_signal(barrier, inc=1, device_id=peer, device_id_type=MESH)

    def rows_of(c, yy, zz):
        return pl.multiple_of(c * half + yy * col_rows + zz * rows, rows)

    mine = rows_of(core, y, z)
    own_x = pltpu.make_async_copy(x_hbm, xg.at[pl.ds(mine, rows), :], own_sem.at[0])
    own_x.start()

    def cols(j):
        return pl.ds(pl.multiple_of(j * width, width), width)

    def up_copy(j):
        return pltpu.make_async_copy(up_hbm.at[0, cols(j), :], up.at[cols(j), :], up_sem.at[j])

    def down_copy(j):
        return pltpu.make_async_copy(down_hbm.at[0, :, cols(j)], down.at[:, cols(j)], down_sem.at[j])

    lax.fori_loop(0, chunks, lambda j, _: (up_copy(j).start(), 0)[1], 0)
    lax.fori_loop(0, chunks, lambda j, _: (down_copy(j).start(), 0)[1], 0)

    lanes = wg.shape[1]
    expert_row = lax.broadcasted_iota(jnp.int32, (lanes, rows), 0)
    spread = jnp.zeros((lanes, rows), jnp.float32)
    for k in range(ids_ref.shape[0]):
        spread += jnp.where(expert_row == ids_ref[k:k + 1, :], weights_ref[k:k + 1, :].astype(jnp.float32), 0.0)
    unit = (lax.broadcasted_iota(jnp.int32, (rows, rows), 0) == lax.broadcasted_iota(jnp.int32, (rows, rows), 1))
    wg[pl.ds(mine, rows), :] = lax.dot_general(
        unit.astype(jnp.float32).astype(jnp.bfloat16), spread.astype(jnp.bfloat16), (((1,), (1,)), ((), ())),
        preferred_element_type=jnp.float32).astype(wg.dtype)

    own_x.wait()
    pl.semaphore_wait(barrier, len(peers))

    def view(start, size, j):
        if j is None:
            return wg.at[pl.ds(start, size), :]
        return xg.at[pl.ds(start, size), cols(j)]

    def idx(j):
        return chunks if j is None else j

    def remote(src, dst, s, r, device):
        return pltpu.make_async_remote_copy(
            src_ref=src, dst_ref=dst, send_sem=s, recv_sem=r, device_id=device, device_id_type=MESH)

    def gz_send(d, j):
        v = view(mine, rows, j)
        return remote(v, v, gz_s.at[d - 1, idx(j)], gz_r.at[d - 1, idx(j)], near(z_plus(d)))

    def direct(d, start):
        if d == 1:
            pl.when(jnp.logical_not(high))(start)
        elif d == last:
            pl.when(jnp.logical_not(low))(start)
        else:
            start()

    def gz_recv(d, j):
        v = view(rows_of(core, y, z_plus(major - d)), rows, j)
        return remote(v, v, gz_s.at[d - 1, idx(j)], gz_r.at[d - 1, idx(j)], near(z_plus(1)))

    far = jnp.where(z == 1, last, 0)
    far_d = jnp.where(z == 1, 2, last - 1)

    def relay(j):
        v = view(rows_of(core, y, far), rows, j)
        d = jnp.where(z == 1, 1, last)
        return remote(v, v, gr_s.at[idx(j)], gz_r.at[d - 1, idx(j)], near(last - far))

    def go(which, j):
        v = view(rows_of(core, which, z), rows, j)
        return remote(v, v, go_s.at[idx(j)], go_r.at[idx(j)], at_y)

    def gy(d, which, j):
        v = view(rows_of(core, which, z_plus(major - d)), rows, j)
        return remote(v, v, gy_s.at[d - 1, idx(j)], gy_r.at[d - 1, idx(j)], at_y)

    def gp(k, c, which, j):
        v = view(rows_of(c, which, 0), col_rows, j)
        return remote(v, v, gp_s.at[k, idx(j)], gp_r.at[k, idx(j)], at_p)

    def stage0(j):
        for d in (*range(2, last), 1, last):
            direct(d, lambda: gz_send(d, j).start())

    def stage_relay(j):
        @pl.when(inner)
        def _():
            gz_recv(far_d, j).wait_recv()
            relay(j).start()

    def stage1(j):
        for d in range(1, major):
            @pl.when(jnp.logical_not(inner & (far_d == d)))
            def _():
                gz_recv(d, j).wait_recv()
            gy(d, y, j).start()
        gp(0, core, y, j).start()

    def stage2(j):
        go(1 - y, j).wait_recv()
        for d in range(1, major):
            gy(d, 1 - y, j).wait_recv()
        gp(1, core, 1 - y, j).start()

    def stage3(j):
        gp(0, 1 - core, y, j).wait_recv()
        gp(1, 1 - core, 1 - y, j).wait_recv()

    lax.fori_loop(0, AHEAD, lambda j, _: (stage0(j), 0)[1], 0)
    lax.fori_loop(0, chunks, lambda j, _: (go(y, j).start(), 0)[1], 0)
    stage0(None)
    go(y, None).start()

    def gather_step(t, _):
        @pl.when(t + AHEAD < chunks)
        def _():
            stage0(t + AHEAD)

        @pl.when(t < chunks)
        def _():
            stage_relay(t)

        @pl.when((t >= LAG_A) & (t < chunks + LAG_A))
        def _():
            stage1(t - LAG_A)

        @pl.when((t >= LAG_B) & (t < chunks + LAG_B))
        def _():
            stage2(t - LAG_B)

        @pl.when(t >= LAG_D)
        def _():
            j = t - LAG_D
            stage3(j)
            up_copy(j).wait()
            for k in range(2):
                r = pl.ds(k * half, half)
                part = jnp.dot(xg[r, cols(j)], up[cols(j), :], preferred_element_type=jnp.float32)

                @pl.when(j == 0)
                def _():
                    acc[r, :] = part

                @pl.when(j > 0)
                def _():
                    acc[r, :] += part
        return 0

    lax.fori_loop(0, chunks, gather_step, 0)
    stage_relay(None)
    lax.fori_loop(chunks, chunks + LAG_A, gather_step, 0)
    stage1(None)
    lax.fori_loop(chunks + LAG_A, chunks + LAG_B, gather_step, 0)
    stage2(None)
    lax.fori_loop(chunks + LAG_B, chunks + LAG_D, gather_step, 0)
    stage3(None)

    for k in range(2):
        r = pl.ds(k * half, half)
        v = acc[r, :]
        hid[r, :] = (v / (1.0 + jnp.exp(-v))).astype(hid.dtype)
    expert = core * (2 * major) + local
    lane = lax.broadcasted_iota(jnp.int32, wg.shape, 1)
    wcol[...] = jnp.sum(jnp.where(lane == expert, wg[...].astype(jnp.float32), 0.0), axis=1, keepdims=True)

    def block(zz):
        return pl.ds(pl.multiple_of(zz * rows, rows), rows)

    def rp(j):
        return remote(psend.at[:, cols(j)], precv.at[:, cols(j)], rp_s.at[j], rp_r.at[j], at_p)

    def ry(d, j):
        r = block(z_plus(d))
        return remote(ysend.at[r, cols(j)], yrecv.at[r, cols(j)], ry_s.at[d - 1, j], ry_r.at[d - 1, j], at_y)

    def ro(j):
        return remote(ysend.at[block(z), cols(j)], yrecv.at[block(z), cols(j)], ro_s.at[j], ro_r.at[j], at_y)

    def rz(d, j):
        return remote(zsend.at[block(z_plus(d)), cols(j)], zrecv.at[d - 1, :, cols(j)],
                      rz_s.at[d - 1, j], rz_r.at[d - 1, j], near(z_plus(d)))

    target = last - z
    via = jnp.where(low, 1, last - 1)
    skip_d = jnp.where(z == 1, last - 1, 2)
    goal = jnp.where(z == 1, last, 0)

    def rr(j):
        return remote(zsend.at[block(target), cols(j)], rin.at[:, cols(j)], rr_s.at[j], rr_r.at[j], near(via))

    theirs = pl.ds(pl.multiple_of((1 - core) * half, half), half)
    ours = pl.ds(pl.multiple_of(core * half, half), half)
    y_theirs = pl.ds(pl.multiple_of((1 - y) * col_rows, col_rows), col_rows)
    y_ours = pl.ds(pl.multiple_of(y * col_rows, col_rows), col_rows)

    def wide(ref, r, j):
        return ref[r, cols(j)].astype(jnp.float32)

    def scatter_step(t, _):
        @pl.when(t < chunks)
        def _():
            j = t
            down_copy(j).wait()
            part = jnp.dot(hid[theirs, :], down[:, cols(j)], preferred_element_type=jnp.float32)
            psend[:, cols(j)] = (part * wcol[theirs, :]).astype(psend.dtype)
            rp(j).start()
            part = jnp.dot(hid[ours, :], down[:, cols(j)], preferred_element_type=jnp.float32)
            pown[:, cols(j)] = part * wcol[ours, :]

        @pl.when((t >= LAG_F) & (t < chunks + LAG_F))
        def _():
            j = t - LAG_F
            rp(j).wait_recv()
            ysend[:, cols(j)] = (pown[y_theirs, cols(j)] + wide(precv, y_theirs, j)).astype(ysend.dtype)
            for d in range(1, major):
                ry(d, j).start()
            yown[:, cols(j)] = pown[y_ours, cols(j)] + wide(precv, y_ours, j)

        @pl.when(t == chunks + LAG_F - 1)
        def _():
            lax.fori_loop(0, chunks, lambda i, _: (ro(i).start(), 0)[1], 0)

        @pl.when((t >= LAG_G) & (t < chunks + LAG_G))
        def _():
            j = t - LAG_G
            for d in range(1, major):
                ry(d, j).wait_recv()
                r = block(z_plus(d))
                zsend[r, cols(j)] = (yown[r, cols(j)] + wide(yrecv, r, j)).astype(zsend.dtype)

            @pl.when(low | high)
            def _():
                rr(j).start()
            for d in range(1, major):
                @pl.when(jnp.logical_not(inner & (skip_d == d)))
                def _():
                    direct(d, lambda: rz(d, j).start())

        @pl.when(inner & (t >= LAG_R) & (t < chunks + LAG_R))
        def _():
            j = t - LAG_R
            rr(j).wait_recv()
            zsend[block(goal), cols(j)] = (
                wide(zsend, block(goal), j) + rin[:, cols(j)].astype(jnp.float32)).astype(zsend.dtype)
            for d in range(1, major):
                @pl.when(skip_d == d)
                def _():
                    rz(d, j).start()
        return 0

    lax.fori_loop(0, chunks + LAG_R, scatter_step, 0)

    def finish(j, _):
        ro(j).wait_recv()
        zown[...] = yown[block(z), cols(j)] + wide(yrecv, block(z), j)
        for d in range(1, major):
            def add():
                rz(d, j).wait_recv()
                zown[...] += zrecv[d - 1, :, cols(j)].astype(jnp.float32)
            if d == 1:
                pl.when(jnp.logical_not(low))(add)
            elif d == last:
                pl.when(jnp.logical_not(high))(add)
            else:
                add()
        out_ref[:, cols(j)] = zown[...].astype(out_ref.dtype)
        return 0

    lax.fori_loop(0, chunks, finish, 0)

    def drain_gather(j):
        for d in range(1, major):
            direct(d, lambda: gz_send(d, j).wait_send())
            gy(d, y, j).wait_send()

        @pl.when(inner)
        def _():
            relay(j).wait_send()
        go(y, j).wait_send()
        gp(0, core, y, j).wait_send()
        gp(1, core, 1 - y, j).wait_send()

    def drain(j, _):
        drain_gather(j)
        rp(j).wait_send()
        ro(j).wait_send()
        for d in range(1, major):
            ry(d, j).wait_send()
            direct(d, lambda: rz(d, j).wait_send())

        @pl.when(low | high)
        def _():
            rr(j).wait_send()
        return 0

    drain_gather(None)
    lax.fori_loop(0, chunks, drain, 0)


def fused(tokens, expert_ids, route_weights, w_up, w_down, width=512):
    rows, depth = tokens.shape
    ff = w_up.shape[2]
    experts = lax.axis_size(("node", "local"))
    major = lax.axis_size("local") // 2
    chunks = depth // width
    lanes = -(-experts // LANES) * LANES
    total, col = experts * rows, major * rows
    half = 2 * col
    bf, f32 = jnp.bfloat16, jnp.float32
    dma = pltpu.SemaphoreType.DMA
    return pl.pallas_call(
        functools.partial(moe_kernel, (rows, major, chunks, width)),
        out_shape=pltpu.VMEM((rows, depth), bf),
        in_specs=[
            pl.BlockSpec(memory_space=pl.ANY),
            pl.BlockSpec(memory_space=pltpu.VMEM),
            pl.BlockSpec(memory_space=pltpu.VMEM),
            pl.BlockSpec(memory_space=pl.ANY),
            pl.BlockSpec(memory_space=pl.ANY),
        ],
        out_specs=pl.BlockSpec(memory_space=pltpu.VMEM),
        scratch_shapes=[
            pltpu.VMEM((total, depth), bf),
            pltpu.VMEM((total, lanes), bf),
            pltpu.VMEM((depth, ff), bf),
            pltpu.VMEM((ff, depth), bf),
            pltpu.VMEM((total, ff), f32),
            pltpu.VMEM((total, ff), bf),
            pltpu.VMEM((total, 1), f32),
            pltpu.VMEM((half, depth), bf),
            pltpu.VMEM((half, depth), f32),
            pltpu.VMEM((half, depth), bf),
            pltpu.VMEM((col, depth), bf),
            pltpu.VMEM((col, depth), f32),
            pltpu.VMEM((col, depth), bf),
            pltpu.VMEM((col, depth), bf),
            pltpu.VMEM((rows, width), f32),
            pltpu.VMEM((major - 1, rows, depth), bf),
            pltpu.VMEM((rows, depth), bf),
            dma((1,)), dma((chunks,)), dma((chunks,)),
            dma((major - 1, chunks + 1)), dma((major - 1, chunks + 1)), dma((chunks + 1,)),
            dma((chunks + 1,)), dma((chunks + 1,)),
            dma((major - 1, chunks + 1)), dma((major - 1, chunks + 1)),
            dma((2, chunks + 1)), dma((2, chunks + 1)),
            dma((chunks,)), dma((chunks,)),
            dma((chunks,)), dma((chunks,)),
            dma((major - 1, chunks)), dma((major - 1, chunks)),
            dma((major - 1, chunks)), dma((major - 1, chunks)),
            dma((chunks,)), dma((chunks,)),
        ],
        compiler_params=pltpu.CompilerParams(
            collective_id=0, has_side_effects=True, vmem_limit_bytes=60 * 1024 * 1024),
    )(tokens, expert_ids.T, route_weights.T, w_up, w_down)


def place_rows(targets, groups, width):
    onehot = (targets[:, None] == jnp.arange(groups, dtype=jnp.int32)[None, :]).astype(jnp.int32)
    before = jnp.cumsum(onehot, axis=0) - onehot
    rank = jnp.sum(before * onehot, axis=1)
    return jnp.where(targets >= 0, targets * width + rank, groups * width)


def per_device(tokens, expert_ids, route_weights, w_up, w_down):
    up_matrix = w_up[0]
    down_matrix = w_down[0]
    rows = tokens.shape[0]
    top = expert_ids.shape[1]
    width_d = tokens.shape[1]
    experts = lax.axis_size(("node", "local"))
    most = max(4, 2 * rows * top // experts)
    slot = place_rows(expert_ids.reshape(-1), experts, most)
    source = tokens[jnp.arange(rows * top, dtype=jnp.int32) // top]
    buffer = jnp.zeros((experts * most, width_d), jnp.bfloat16).at[slot].set(source, mode="drop")
    buffer = buffer.reshape(experts, most, width_d)
    received = lax.all_to_all(buffer, ("node", "local"), split_axis=0, concat_axis=0, tiled=True)
    shape = received.shape
    flat = received.reshape(-1, shape[-1])
    hidden = jax.nn.silu(jnp.dot(flat, up_matrix, preferred_element_type=jnp.float32)).astype(
        jnp.bfloat16
    )
    answer = jnp.dot(hidden, down_matrix, preferred_element_type=jnp.float32).astype(jnp.bfloat16)
    done = answer.reshape(shape)
    returned = lax.all_to_all(
        done, ("node", "local"), split_axis=0, concat_axis=0, tiled=True
    ).reshape(experts * most, width_d)
    picked = returned[jnp.minimum(slot, experts * most - 1)].reshape(rows, top, width_d)
    mixed = jnp.einsum("tk,tkd->td", route_weights, picked, preferred_element_type=jnp.float32)
    return mixed.astype(jnp.bfloat16)


def solution(mesh):
    placed = (
        P(("rep", "node", "local"), None),
        P(("rep", "node", "local"), None),
        P(("rep", "node", "local"), None),
        P(("node", "local"), None, None),
        P(("node", "local"), None, None),
    )

    def body(tokens, expert_ids, route_weights, w_up, w_down):
        experts = mesh.shape["node"] * mesh.shape["local"]
        near_dense = experts <= 2 * expert_ids.shape[1]
        if near_dense and mesh.shape["node"] == 2 and mesh.shape["local"] % 2 == 0 and mesh.shape["local"] >= 8:
            return fused(tokens, expert_ids, route_weights, w_up, w_down)
        return per_device(tokens, expert_ids, route_weights, w_up, w_down)

    return jax.shard_map(
        body,
        mesh=mesh,
        in_specs=placed,
        out_specs=P(("rep", "node", "local"), None),
        check_vma=False,
    )
```

profile of v0, /device:TPU:0, one launch (start us, length us, event | category | flops | bytes accessed | tf_op | source)
XLA Modules:
  0.0 59.8 jit_solution(12389131259999789891)
XLA Ops:
  0.0 59.1 %shard_map.55 = bf16[32,3584]{1,0:T(8,128)(2,1)S(1)} custom-call(bf16[32,3584]{1,0:T(8,128)(2,1)} %x_hbm.1, s32[8,32]{1,0:T(8,128)} %bitcast.2, bf16[8,32]{1,0:T(8,128)(2,1)} %bitcast.3, bf16[1,3584,1024]{2,1,0:T(8,128)(2,1)} %up_hbm.1, bf16[1,1024,3584]{2,1,0:T(8,128)(2,1)} %down_hbm.1), custom_call_target="tpu_custom_call" | custom-call | tf_op jit(solution)/shard_map/pallas_call | solution.py:355
  59.1 0.7 %copy.7 = bf16[32,3584]{1,0:T(8,128)(2,1)} copy(bf16[32,3584]{1,0:T(8,128)(2,1)S(1)} %shard_map.55) | data formatting | bytes 458752
where the time goes:
time: 59.9 us; the launch traced here: 59.8 us
  Pallas kernels  59.1 us (99%)
  local copies, waits for them, and re-layouts  0.69 us (1%)
    pallas_call x1, Pallas kernels, fused(): pl.pallas_call(functools.partial(moe_kernel, (rows, major, chunks, width)...  59.1 us

commit v1 on v0

v1 whole, which is shorter than its diff:
```python
import functools
import jax
import jax.numpy as jnp
from jax import lax
from jax.experimental import pallas as pl
from jax.experimental.pallas import tpu as pltpu
from jax.sharding import PartitionSpec as P

MESH = pl.DeviceIdType.MESH
LANES = 128
AHEAD_Z = 2
AHEAD_Y = 10
TABLE = 3
LAG_B = -2
LAG_A = (1, 1, 3)
LAG_P = (5, 6)
LAG_C = 7
LAG_E = 2
LAG_F = 5
LAG_G = 7
LAG_S = 9
LAG_FIN = 9
SWAP_G = ((),())
SWAP_R = ((),())


def moe_kernel(sizes, x_hbm, ids_ref, weights_ref, up_hbm, down_hbm, out_ref,
               xg, wg, up, down, acc, hid, psend, precv, pown, ysend, yrecv, zs, zr,
               own_sem, up_sem, down_sem,
               gz_s, gz_r, gy_s, gy_r, gp_s, gp_r,
               rp_s, rp_r, ry_s, ry_r, rz_s, rz_r):
    rows, major, chunks, width = sizes
    core = lax.axis_index("node")
    local = lax.axis_index("local")
    z, y = local // 2, lax.rem(local, 2)
    last = major - 1
    hr = rows // 2
    col = major * hr
    half = 2 * col
    grp = 2 * half
    nq = 2 * chunks
    f32 = jnp.float32

    up_z, down_z = jnp.minimum(z + 1, last), jnp.maximum(z - 1, 0)
    cross = lax.rem(z + 2, major)
    nexts = ({"local": up_z * 2 + y}, {"local": down_z * 2 + y}, {"local": cross * 2 + y})
    corner = (z == 0) | (z == last)
    far = last - z
    inward = {"local": jnp.where(z == 0, 1, last - 1) * 2 + y}
    outward = {"local": jnp.where(z == 1, 0, last) * 2 + y}
    at_y = {"local": z * 2 + (1 - y)}
    at_p = {"node": 1 - core}
    has = (z < last, z > 0, z >= 0)
    came = (z > 0, z < last, z >= 0, corner)
    block_of = (down_z, up_z, cross, far)

    barrier = pltpu.get_barrier_semaphore()
    peers = [{"local": lax.rem(z + d, major) * 2 + y} for d in range(1, major)] + [at_y, at_p]
    for peer in peers:
        pl.semaphore_signal(barrier, inc=1, device_id=peer, device_id_type=MESH)

    def zrow(zz):
        return pl.multiple_of(zz * hr, hr)

    own_x = []
    for h in range(2):
        own_x.append(pltpu.make_async_copy(
            x_hbm.at[pl.ds(h * hr, hr), :], xg.at[h, 0, pl.ds(zrow(z), hr), :], own_sem.at[h]))
        own_x[h].start()

    def cols(j):
        return pl.ds(pl.multiple_of(j * width, width), width)

    def up_copy(j):
        return pltpu.make_async_copy(up_hbm.at[0, cols(j), :], up.at[cols(j), :], up_sem.at[j])

    def down_copy(j):
        return pltpu.make_async_copy(down_hbm.at[0, :, cols(j)], down.at[:, cols(j)], down_sem.at[j])

    lax.fori_loop(0, chunks, lambda j, _: (up_copy(j).start(), 0)[1], 0)
    lax.fori_loop(0, chunks, lambda j, _: (down_copy(j).start(), 0)[1], 0)

    lanes = wg.shape[3]
    expert_row = lax.broadcasted_iota(jnp.int32, (lanes, rows), 0)
    spread = jnp.zeros((lanes, rows), f32)
    for k in range(ids_ref.shape[0]):
        spread += jnp.where(expert_row == ids_ref[k:k + 1, :], weights_ref[k:k + 1, :].astype(f32), 0.0)
    unit = (lax.broadcasted_iota(jnp.int32, (rows, rows), 0) == lax.broadcasted_iota(jnp.int32, (rows, rows), 1))
    table = lax.dot_general(
        unit.astype(f32).astype(jnp.bfloat16), spread.astype(jnp.bfloat16), (((1,), (1,)), ((), ())),
        preferred_element_type=f32).astype(wg.dtype)
    for h in range(2):
        wg[h, 0, pl.ds(zrow(z), hr), :] = table[h * hr:(h + 1) * hr, :]

    for h in range(2):
        own_x[h].wait()
    pl.semaphore_wait(barrier, len(peers))

    def split(q):
        h = (q >= chunks).astype(jnp.int32)
        return h, q - h * chunks

    def swapped(q, sets):
        if q is None:
            return jnp.bool_(False)
        out = jnp.bool_(False)
        for s in range(2):
            for k in sets[s]:
                out = out | (q == s * chunks + k)
        return out

    def count(sets):
        return len(sets[0]) + len(sets[1])

    def region(q, a, n, zz, size):
        if q is None:
            return wg.at[:, pl.ds(a, n), pl.ds(zrow(zz), size), :]
        h, j = split(q)
        return xg.at[h, pl.ds(a, n), pl.ds(zrow(zz), size), cols(j)]

    def idx(q):
        return nq if q is None else q

    def kind(q):
        return 1 if q is None else 0

    def remote(src, dst, s, r, device):
        return pltpu.make_async_remote_copy(
            src_ref=src, dst_ref=dst, send_sem=s, recv_sem=r, device_id=device, device_id_type=MESH)

    def sent(sem, ref):
        remote(ref, ref, sem, sem, at_p).wait_send()

    def gz(slot, n, q):
        v = region(q, 0, n, z, hr)
        return remote(v, v, gz_s.at[slot, kind(q)], gz_r.at[slot, idx(q)], nexts[slot])

    def relay(n, q):
        v = region(q, 0, n, cross, hr)
        return remote(v, v, gz_s.at[3, kind(q)], gz_r.at[3, idx(q)], outward)

    def gz_in(slot, n, q):
        v = region(q, 0, n, block_of[slot], hr)
        return remote(v, v, gz_s.at[slot, kind(q)], gz_r.at[slot, idx(q)], nexts[2])

    def gy(zz, q, own):
        return remote(region(q, 0, 1, zz, hr), region(q, 1, 1, zz, hr), gy_s.at[own, kind(q)], gy_r.at[idx(q)], at_y)

    def gy_in(zz, size, q):
        v = region(q, 1, 1, zz, size)
        return remote(v, v, gy_s.at[0, kind(q)], gy_r.at[idx(q)], at_y)

    def gp(k, q):
        return remote(region(q, k, 1, 0, col), region(q, 2 + k, 1, 0, col), gp_s.at[kind(q)], gp_r.at[idx(q)], at_p)

    def gp_in(q):
        v = region(q, 2, 2, 0, col)
        return remote(v, v, gp_s.at[kind(q)], gp_r.at[idx(q)], at_p)

    def plain(q, fn):
        if q is None:
            fn()
        else:
            pl.when(jnp.logical_not(swapped(q, SWAP_G)))(fn)

    def twice(q, fn):
        if q is not None and count(SWAP_G):
            pl.when(swapped(q, SWAP_G))(fn)

    def start_z(n, q):
        gz(2, n, q).start()
        for d in range(2):
            @pl.when(has[d])
            def _():
                gz(d, n, q).start()

    def stage0z(q):
        plain(q, lambda: start_z(1, q))

    def stage0y(q):
        gy(z, q, 1).start()

    def stage_b(q):
        def go():
            gy_in(z, hr, q).wait_recv()
            start_z(2, q)
        twice(q, go)

    def stage_a(slots, q):
        def step(n):
            for slot in slots:
                @pl.when(came[slot])
                def _():
                    gz_in(slot, n, q).wait_recv()
                    if slot == 2:
                        @pl.when(jnp.logical_not(corner))
                        def _():
                            relay(n, q).start()
                    if n == 1:
                        gy(block_of[slot], q, 0).start()
        plain(q, lambda: step(1))
        twice(q, lambda: step(2))

    def stage_p(k, q):
        if k == 1:
            plain(q, lambda: gy_in(0, col, q).wait_recv())
        gp(k, q).start()

    def stage_in(q):
        gp_in(q).wait_recv()

    expert = core * (2 * major) + local

    def stage_c(q):
        stage_in(q)
        h, j = split(q)

        @pl.when(h == 0)
        def _():
            up_copy(j).wait()
        x = xg[h, :, :, cols(j)].reshape(grp, width)
        part = jnp.dot(x, up[cols(j), :], preferred_element_type=f32)

        @pl.when(j == 0)
        def _():
            acc[...] = part

        @pl.when(j > 0)
        def _():
            acc[...] += part

        @pl.when(j == chunks - 1)
        def _():
            lane = lax.broadcasted_iota(jnp.int32, (grp, lanes), 1)
            table = wg[h].reshape(grp, lanes).astype(f32)
            weight = jnp.sum(jnp.where(lane == expert, table, 0.0), axis=1, keepdims=True)
            v = acc[...]
            hid[h] = (v / (1.0 + jnp.exp(-v)) * weight).astype(hid.dtype)

    def rp(r):
        h, j = split(r)
        return remote(psend.at[h, :, :, cols(j)], precv.at[h, :, :, cols(j)], rp_s.at[0], rp_r.at[r], at_p)

    def ry(size, r):
        h, j = split(r)
        return remote(ysend.at[h, pl.ds(0, size), cols(j)], yrecv.at[h, pl.ds(0, size), cols(j)],
                      ry_s.at[0], ry_r.at[r], at_y)

    def rz(slot, n, zz, r):
        h, j = split(r)
        return remote(zs.at[h, pl.ds(0, n), pl.ds(zrow(zz), hr), cols(j)],
                      zr.at[slot, h, pl.ds(0, n), :, cols(j)], rz_s.at[slot], rz_r.at[slot, r],
                      nexts[slot] if slot < 3 else inward)

    def plain_r(r, fn):
        pl.when(jnp.logical_not(swapped(r, SWAP_R)))(fn)

    def twice_r(r, fn):
        if count(SWAP_R):
            pl.when(swapped(r, SWAP_R))(fn)

    def stage_d(r):
        h, j = split(r)

        @pl.when(h == 0)
        def _():
            down_copy(j).wait()
        part = jnp.dot(hid[h], down[:, cols(j)], preferred_element_type=f32)
        psend[h, :, :, cols(j)] = part[half:, :].astype(psend.dtype).reshape(2, col, width)
        rp(r).start()
        pown[h, :, :, cols(j)] = part[:half, :].reshape(2, col, width)

    def stage_e(r):
        h, j = split(r)
        rp(r).wait_recv()

        def one():
            ysend[h, :, cols(j)] = (pown[h, 1, :, cols(j)] + precv[h, 1, :, cols(j)].astype(f32)).astype(ysend.dtype)
            ry(col, r).start()

        def two():
            pown[h, 1, :, cols(j)] += precv[h, 1, :, cols(j)].astype(f32)
        plain_r(r, one)
        twice_r(r, two)
        pown[h, 0, :, cols(j)] += precv[h, 0, :, cols(j)].astype(f32)

    def spread_z(m, r):
        h, j = split(r)
        v = (h, pl.ds(0, m), slice(None), cols(j))
        zs[v] = pown[v].astype(zs.dtype)

        @pl.when(corner)
        def _():
            rz(3, m, far, r).start()
            rz(2, m, cross, r).start()
        for slot in range(2):
            @pl.when(has[slot])
            def _():
                rz(slot, m, (up_z, down_z)[slot], r).start()

    def stage_f(r):
        h, j = split(r)

        def one():
            ry(col, r).wait_recv()
            pown[h, 0, :, cols(j)] += yrecv[h, :, cols(j)].astype(f32)
            spread_z(1, r)
        plain_r(r, one)
        twice_r(r, lambda: spread_z(2, r))

    def stage_g(r):
        h, j = split(r)

        def flow(m):
            rz(3, m, cross, r).wait_recv()
            v = (h, pl.ds(0, m), pl.ds(zrow(cross), hr), cols(j))
            zs[v] = (pown[v] + zr[3, h, pl.ds(0, m), :, cols(j)].astype(f32)).astype(zs.dtype)
            rz(2, m, cross, r).start()

        @pl.when(jnp.logical_not(corner))
        def _():
            plain_r(r, lambda: flow(1))
            twice_r(r, lambda: flow(2))

    def settle(m, r):
        h, j = split(r)
        v = (h, pl.ds(0, m), pl.ds(zrow(z), hr), cols(j))
        for slot in range(3):
            @pl.when(came[slot])
            def _():
                rz(slot, m, z, r).wait_recv()
                pown[v] += zr[slot, h, pl.ds(0, m), :, cols(j)].astype(f32)

    def stage_s(r):
        h, j = split(r)
        mine = pl.ds(zrow(z), hr)

        def two():
            settle(2, r)
            ysend[h, pl.ds(0, hr), cols(j)] = pown[h, 1, mine, cols(j)].astype(ysend.dtype)
            ry(hr, r).start()
        plain_r(r, lambda: settle(1, r))
        twice_r(r, two)

    def stage_fin(r):
        h, j = split(r)
        mine = pl.ds(zrow(z), hr)
        out = pl.ds(pl.multiple_of(h * hr, hr), hr)

        def one():
            out_ref[out, cols(j)] = pown[h, 0, mine, cols(j)].astype(out_ref.dtype)

        def two():
            ry(hr, r).wait_recv()
            out_ref[out, cols(j)] = (
                pown[h, 0, mine, cols(j)] + yrecv[h, pl.ds(0, hr), cols(j)].astype(f32)).astype(out_ref.dtype)
        plain_r(r, one)
        twice_r(r, two)

    gather = [(stage_b, LAG_B)]
    gather += [(functools.partial(stage_a, s), lag) for s, lag in zip(((0, 1), (2,), (3,)), LAG_A)]
    gather += [(functools.partial(stage_p, k), LAG_P[k]) for k in range(2)]
    start_r = LAG_C + chunks - 1
    reduce_a = [(stage_e, start_r + LAG_E), (stage_f, start_r + LAG_F), (stage_g, start_r + LAG_G),
                (stage_s, start_r + LAG_S), (stage_fin, start_r + LAG_FIN)]
    late = start_r + LAG_FIN

    def run(t, stages):
        for fn, lag in stages:
            @pl.when((t >= lag) & (t < nq + lag))
            def _():
                fn(t - lag)

    def early(t):
        @pl.when(t + AHEAD_Z < nq)
        def _():
            stage0z(t + AHEAD_Z)

        @pl.when(t + AHEAD_Y < nq)
        def _():
            stage0y(t + AHEAD_Y)
        for fn, lag in gather[1:] + [(stage_in, LAG_C)]:
            @pl.when(t == TABLE + lag)
            def _():
                fn(None)
        run(t, gather)

    def first(t, _):
        early(t)
        run(t, [(stage_c, LAG_C)])
        return 0

    def middle(t, _):
        early(t)
        run(t, reduce_a)
        run(t, [(stage_c, LAG_C), (stage_d, start_r)])
        return 0

    def final(t, _):
        run(t, reduce_a)
        run(t, [(stage_d, start_r)])
        return 0

    lax.fori_loop(0, AHEAD_Z, lambda q, _: (stage0z(q), 0)[1], 0)
    lax.fori_loop(0, AHEAD_Y, lambda q, _: (stage0y(q), 0)[1], 0)
    stage0z(None)
    stage0y(None)
    lax.fori_loop(0, start_r, first, 0)
    lax.fori_loop(start_r, nq + LAG_C, middle, 0)
    lax.fori_loop(nq + LAG_C, nq + late, final, 0)

    def whole(sem, blocks):
        while blocks:
            n = min(blocks, 4 * chunks)
            r = n if n < 4 else n - n % 4
            if n < 4:
                ref = xg.at[0, pl.ds(0, 1), pl.ds(0, hr), pl.ds(0, n * width)]
            else:
                ref = xg.at[0, pl.ds(0, 1), pl.ds(0, col), pl.ds(0, r // 4 * width)]
            sent(sem, ref)
            blocks -= r

    ng, nr = count(SWAP_G), count(SWAP_R)
    whole(gy_s.at[1, 0], nq)
    whole(gy_s.at[0, 0], (nq - ng) * last)
    whole(gp_s.at[0], nq * 2 * major)
    for slot in range(4):
        @pl.when((*has, jnp.logical_not(corner))[slot])
        def _():
            whole(gz_s.at[slot, 0], nq + ng)
            sent(gz_s.at[slot, 1], wg.at[:, pl.ds(0, 1), pl.ds(0, hr), :])
    sent(gy_s.at[1, 1], wg.at[:, pl.ds(0, 1), pl.ds(0, hr), :])
    sent(gy_s.at[0, 1], wg.at[:, pl.ds(0, 1), pl.ds(0, last * hr), :])
    sent(gp_s.at[1], wg.at[:, pl.ds(0, 2), pl.ds(0, col), :])
    whole(rp_s.at[0], nq * 2 * major)
    whole(ry_s.at[0], (nq - nr) * major + nr)
    for slot in range(4):
        @pl.when((*has, corner)[slot])
        def _():
            whole(rz_s.at[slot], nq + nr)


def fused(tokens, expert_ids, route_weights, w_up, w_down, width=512):
    rows, depth = tokens.shape
    ff = w_up.shape[2]
    experts = lax.axis_size(("node", "local"))
    major = lax.axis_size("local") // 2
    chunks = depth // width
    lanes = -(-experts // LANES) * LANES
    col = major * rows // 2
    bf, f32 = jnp.bfloat16, jnp.float32
    nq = 2 * chunks
    dma = pltpu.SemaphoreType.DMA
    return pl.pallas_call(
        functools.partial(moe_kernel, (rows, major, chunks, width)),
        out_shape=pltpu.VMEM((rows, depth), bf),
        in_specs=[
            pl.BlockSpec(memory_space=pl.ANY),
            pl.BlockSpec(memory_space=pltpu.VMEM),
            pl.BlockSpec(memory_space=pltpu.VMEM),
            pl.BlockSpec(memory_space=pl.ANY),
            pl.BlockSpec(memory_space=pl.ANY),
        ],
        out_specs=pl.BlockSpec(memory_space=pltpu.VMEM),
        scratch_shapes=[
            pltpu.VMEM((2, 4, col, depth), bf),
            pltpu.VMEM((2, 4, col, lanes), bf),
            pltpu.VMEM((depth, ff), bf),
            pltpu.VMEM((ff, depth), bf),
            pltpu.VMEM((4 * col, ff), f32),
            pltpu.VMEM((2, 4 * col, ff), bf),
            pltpu.VMEM((2, 2, col, depth), bf),
            pltpu.VMEM((2, 2, col, depth), bf),
            pltpu.VMEM((2, 2, col, depth), f32),
            pltpu.VMEM((2, col, depth), bf),
            pltpu.VMEM((2, col, depth), bf),
            pltpu.VMEM((2, 2, col, depth), bf),
            pltpu.VMEM((4, 2, 2, rows // 2, depth), bf),
            dma((2,)), dma((chunks,)), dma((chunks,)),
            dma((4, 2)), dma((4, nq + 1)),
            dma((2, 2)), dma((nq + 1,)),
            dma((2,)), dma((nq + 1,)),
            dma((1,)), dma((nq,)),
            dma((1,)), dma((nq,)),
            dma((4,)), dma((4, nq)),
        ],
        compiler_params=pltpu.CompilerParams(
            collective_id=0, has_side_effects=True, vmem_limit_bytes=60 * 1024 * 1024),
    )(tokens, expert_ids.T, route_weights.T, w_up, w_down)


def place_rows(targets, groups, width):
    onehot = (targets[:, None] == jnp.arange(groups, dtype=jnp.int32)[None, :]).astype(jnp.int32)
    before = jnp.cumsum(onehot, axis=0) - onehot
    rank = jnp.sum(before * onehot, axis=1)
    return jnp.where(targets >= 0, targets * width + rank, groups * width)


def per_device(tokens, expert_ids, route_weights, w_up, w_down):
    up_matrix = w_up[0]
    down_matrix = w_down[0]
    rows = tokens.shape[0]
    top = expert_ids.shape[1]
    width_d = tokens.shape[1]
    experts = lax.axis_size(("node", "local"))
    most = max(4, 2 * rows * top // experts)
    slot = place_rows(expert_ids.reshape(-1), experts, most)
    source = tokens[jnp.arange(rows * top, dtype=jnp.int32) // top]
    buffer = jnp.zeros((experts * most, width_d), jnp.bfloat16).at[slot].set(source, mode="drop")
    buffer = buffer.reshape(experts, most, width_d)
    received = lax.all_to_all(buffer, ("node", "local"), split_axis=0, concat_axis=0, tiled=True)
    shape = received.shape
    flat = received.reshape(-1, shape[-1])
    hidden = jax.nn.silu(jnp.dot(flat, up_matrix, preferred_element_type=jnp.float32)).astype(
        jnp.bfloat16
    )
    answer = jnp.dot(hidden, down_matrix, preferred_element_type=jnp.float32).astype(jnp.bfloat16)
    done = answer.reshape(shape)
    returned = lax.all_to_all(
        done, ("node", "local"), split_axis=0, concat_axis=0, tiled=True
    ).reshape(experts * most, width_d)
    picked = returned[jnp.minimum(slot, experts * most - 1)].reshape(rows, top, width_d)
    mixed = jnp.einsum("tk,tkd->td", route_weights, picked, preferred_element_type=jnp.float32)
    return mixed.astype(jnp.bfloat16)


def solution(mesh):
    placed = (
        P(("rep", "node", "local"), None),
        P(("rep", "node", "local"), None),
        P(("rep", "node", "local"), None),
        P(("node", "local"), None, None),
        P(("node", "local"), None, None),
    )

    def body(tokens, expert_ids, route_weights, w_up, w_down):
        experts = mesh.shape["node"] * mesh.shape["local"]
        near_dense = experts <= 2 * expert_ids.shape[1]
        if near_dense and mesh.shape["node"] == 2 and mesh.shape["local"] == 8:
            return fused(tokens, expert_ids, route_weights, w_up, w_down)
        return per_device(tokens, expert_ids, route_weights, w_up, w_down)

    return jax.shard_map(
        body,
        mesh=mesh,
        in_specs=placed,
        out_specs=P(("rep", "node", "local"), None),
        check_vma=False,
    )
```

time: 59.9 us -> 57.9 us (0.967)
  Pallas kernels: 59.1 us -> 57 us
    pallas_call x1, Pallas kernels: 59.1 us -> 57 us  [fused(): pl.pallas_call(functools.partial(moe_kernel, (rows, major, chunks, width)...]
where the time goes in v1:
time: 57.9 us; the launch traced here: 57.7 us
  Pallas kernels  57 us (98%)
  local copies, waits for them, and re-layouts  0.69 us (1%)
    pallas_call x1, Pallas kernels, fused(): pl.pallas_call(functools.partial(moe_kernel, (rows, major, chunks, width)...  57 us

profile of v1, /device:TPU:0, one launch (start us, length us, event | category | flops | bytes accessed | tf_op | source)
XLA Modules:
  0.0 57.7 jit_solution(16484656750817988203)
XLA Ops:
  0.0 57.0 %shard_map.55 = bf16[32,3584]{1,0:T(8,128)(2,1)S(1)} custom-call(bf16[32,3584]{1,0:T(8,128)(2,1)} %x_hbm.1, s32[8,32]{1,0:T(8,128)} %bitcast.2, bf16[8,32]{1,0:T(8,128)(2,1)} %bitcast.3, bf16[1,3584,1024]{2,1,0:T(8,128)(2,1)} %up_hbm.1, bf16[1,1024,3584]{2,1,0:T(8,128)(2,1)} %down_hbm.1), custom_call_target="tpu_custom_call" | custom-call | tf_op jit(solution)/shard_map/pallas_call | solution.py:454
  57.1 0.7 %copy.7 = bf16[32,3584]{1,0:T(8,128)(2,1)} copy(bf16[32,3584]{1,0:T(8,128)(2,1)S(1)} %shard_map.55) | data formatting | bytes 458752

commit v2 on v1

v2 whole, which is shorter than its diff:
```python
import functools
import jax
import jax.numpy as jnp
from jax import lax
from jax.experimental import pallas as pl
from jax.experimental.pallas import tpu as pltpu
from jax.sharding import PartitionSpec as P

MESH = pl.DeviceIdType.MESH
LANES = 128
AHEAD_Z = 2
AHEAD_Y = 10
TABLE = 3
LAG_A = (1, 1, 3)
LAG_P = (5, 6)
LAG_C = 7
LAG_E = 2
LAG_F = 5
LAG_G = 8
LAG_S = 11
DEFER = 10
DIRECT = 3


def moe_kernel(sizes, x_hbm, ids_ref, weights_ref, up_hbm, down_hbm, out_ref,
               xg, wg, up, down, acc, hid, psend, precv, pown, ysend, yrecv, zs, zr,
               own_sem, up_sem, down_sem,
               gz_s, gz_r, gy_s, gy_r, gp_s, gp_r,
               rp_s, rp_r, ry_s, ry_r, ro_s, ro_r, rz_s, rz_r):
    rows, major, chunks, width = sizes
    core = lax.axis_index("node")
    local = lax.axis_index("local")
    z, y = local // 2, lax.rem(local, 2)
    last = major - 1
    hr = rows // 2
    col = major * hr
    half = 2 * col
    grp = 2 * half
    nq = 2 * chunks
    f32 = jnp.float32

    up_z, down_z = jnp.minimum(z + 1, last), jnp.maximum(z - 1, 0)
    cross = lax.rem(z + 2, major)
    corner = (z == 0) | (z == last)
    far = jnp.where(corner, last - z, cross)
    nexts = tuple({"local": zz * 2 + y} for zz in (up_z, down_z, cross, far))
    inward = {"local": jnp.where(z == 0, 1, last - 1) * 2 + y}
    outward = {"local": jnp.where(z == 1, 0, last) * 2 + y}
    at_y = {"local": z * 2 + (1 - y)}
    at_p = {"node": 1 - core}
    has = (z < last, z > 0, z >= 0)
    came = (z > 0, z < last, z >= 0, corner)
    from_rel = (last, 1, 2, jnp.where(z == 0, last, 1))
    to_rel = (1, last, 2, jnp.where(z == 0, last, 1))
    relay_rel = jnp.where(z == 1, last, 1)

    barrier = pltpu.get_barrier_semaphore()
    peers = [{"local": lax.rem(z + d, major) * 2 + y} for d in range(1, major)] + [at_y, at_p]
    for peer in peers:
        pl.semaphore_signal(barrier, inc=1, device_id=peer, device_id_type=MESH)

    def rel(k, n=1):
        return pl.ds(k * hr if isinstance(k, int) else pl.multiple_of(k * hr, hr), n * hr)

    own_x = []
    for h in range(2):
        own_x.append(pltpu.make_async_copy(
            x_hbm.at[pl.ds(h * hr, hr), :], xg.at[h, 0, rel(0), :], own_sem.at[h]))
        own_x[h].start()

    def cols(j):
        return pl.ds(pl.multiple_of(j * width, width), width)

    def up_copy(j):
        return pltpu.make_async_copy(up_hbm.at[0, cols(j), :], up.at[cols(j), :], up_sem.at[j])

    def down_copy(j):
        return pltpu.make_async_copy(down_hbm.at[0, :, cols(j)], down.at[:, cols(j)], down_sem.at[j])

    lax.fori_loop(0, chunks, lambda j, _: (up_copy(j).start(), 0)[1], 0)
    lax.fori_loop(0, chunks, lambda j, _: (down_copy(j).start(), 0)[1], 0)

    pl.semaphore_wait(barrier, len(peers))

    def split(q):
        h = (q >= chunks).astype(jnp.int32)
        return h, q - h * chunks

    def region(q, a, n, k, m):
        if q is None:
            return wg.at[:, pl.ds(a, n), rel(k, m), :]
        h, j = split(q)
        return xg.at[h, pl.ds(a, n), rel(k, m), cols(j)]

    def idx(q):
        return nq if q is None else q

    def kind(q):
        return 1 if q is None else 0

    def remote(src, dst, s, r, device):
        return pltpu.make_async_remote_copy(
            src_ref=src, dst_ref=dst, send_sem=s, recv_sem=r, device_id=device, device_id_type=MESH)

    def sent(sem, ref):
        remote(ref, ref, sem, sem, at_p).wait_send()

    def own(q, a, k):
        if q is None:
            return wg.at[:, 0, rel(0), :], wg.at[:, a, rel(k), :]
        h, j = split(q)
        return x_hbm.at[pl.ds(pl.multiple_of(h * hr, hr), hr), cols(j)], xg.at[h, a, rel(k), cols(j)]

    def gz(slot, q):
        return remote(*own(q, 0, from_rel[slot]), gz_s.at[slot, kind(q)], gz_r.at[slot, idx(q)], nexts[slot])

    def relay(q):
        return remote(region(q, 0, 1, 2, 1), region(q, 0, 1, relay_rel, 1),
                      gz_s.at[3, kind(q)], gz_r.at[3, idx(q)], outward)

    def gz_in(slot, q):
        v = region(q, 0, 1, from_rel[slot], 1)
        return remote(v, v, gz_s.at[slot, kind(q)], gz_r.at[slot, idx(q)], nexts[2])

    def gy(k, q):
        v = own(q, 1, 0) if k is None else (region(q, 0, 1, k, 1), region(q, 1, 1, k, 1))
        return remote(*v, gy_s.at[int(k is None), kind(q)], gy_r.at[idx(q)], at_y)

    def gy_in(q):
        v = region(q, 1, 1, 0, major)
        return remote(v, v, gy_s.at[0, kind(q)], gy_r.at[idx(q)], at_y)

    def gp(k, q):
        return remote(region(q, k, 1, 0, major), region(q, 2 + k, 1, 0, major), gp_s.at[kind(q)], gp_r.at[idx(q)], at_p)

    def gp_in(q):
        v = region(q, 2, 2, 0, major)
        return remote(v, v, gp_s.at[kind(q)], gp_r.at[idx(q)], at_p)

    def stage0z(q):
        gz(2, q).start()
        for d in range(2):
            @pl.when(has[d])
            def _():
                gz(d, q).start()

    def stage0y(q):
        gy(None, q).start()

    def stage_a(slots, q):
        for slot in slots:
            @pl.when(came[slot])
            def _():
                gz_in(slot, q).wait_recv()
                if slot == 2:
                    @pl.when(jnp.logical_not(corner))
                    def _():
                        relay(q).start()
                gy(from_rel[slot], q).start()

    def stage_p(k, q):
        if k == 1:
            gy_in(q).wait_recv()
        gp(k, q).start()

    def stage_in(q):
        gp_in(q).wait_recv()

    lanes = wg.shape[3]
    expert = core * (2 * major) + local

    def stage_c(q):
        stage_in(q)
        h, j = split(q)

        @pl.when(h == 0)
        def _():
            up_copy(j).wait()
        x = xg[h, :, :, cols(j)].reshape(grp, width)
        part = jnp.dot(x, up[cols(j), :], preferred_element_type=f32)

        @pl.when(j == 0)
        def _():
            acc[...] = part

        @pl.when(j > 0)
        def _():
            acc[...] += part

        @pl.when(j == chunks - 1)
        def _():
            lane = lax.broadcasted_iota(jnp.int32, (grp, lanes), 1)
            table = wg[h].reshape(grp, lanes).astype(f32)
            weight = jnp.sum(jnp.where(lane == expert, table, 0.0), axis=1, keepdims=True)
            v = acc[...]
            hid[h] = (v / (1.0 + jnp.exp(-v)) * weight).astype(hid.dtype)

    def rp(r):
        h, j = split(r)
        return remote(psend.at[h, :, :, cols(j)], precv.at[h, :, :, cols(j)], rp_s.at[0], rp_r.at[r], at_p)

    def ry(r):
        h, j = split(r)
        v = (h, rel(1, last), cols(j))
        return remote(ysend.at[v], yrecv.at[v], ry_s.at[0], ry_r.at[r], at_y)

    def ro(r):
        h, j = split(r)
        v = (h, rel(0), cols(j))
        return remote(ysend.at[v], yrecv.at[v], ro_s.at[0], ro_r.at[r], at_y)

    def rz(slot, r):
        h, j = split(r)
        return remote(zs.at[h, rel(to_rel[slot]), cols(j)], zr.at[slot, h, :, cols(j)],
                      rz_s.at[slot], rz_r.at[slot, r], nexts[slot])

    def rr(r):
        h, j = split(r)
        return remote(zs.at[h, rel(to_rel[3]), cols(j)], zr.at[3, h, :, cols(j)], rz_s.at[3], rz_r.at[3, r], inward)

    def stage_d(r):
        h, j = split(r)

        @pl.when(h == 0)
        def _():
            down_copy(j).wait()
        part = jnp.dot(hid[h], down[:, cols(j)], preferred_element_type=f32)
        psend[h, :, :, cols(j)] = part[half:, :].astype(psend.dtype).reshape(2, col, width)
        rp(r).start()
        pown[h, :, :, cols(j)] = part[:half, :].reshape(2, col, width)

    def stage_e(r):
        h, j = split(r)
        rp(r).wait_recv()
        ysend[h, :, cols(j)] = (pown[h, 1, :, cols(j)] + precv[h, 1, :, cols(j)].astype(f32)).astype(ysend.dtype)
        ry(r).start()

        @pl.when(r < nq - DEFER)
        def _():
            ro(r).start()
        pown[h, 0, :, cols(j)] += precv[h, 0, :, cols(j)].astype(f32)

        @pl.when(r == nq - 1)
        def _():
            lax.fori_loop(nq - DEFER, nq, lambda k, _: (ro(k).start(), 0)[1], 0)

    def stage_f(r):
        h, j = split(r)
        ry(r).wait_recv()
        v = (h, rel(1, last), cols(j))
        zs[v] = (pown[h, 0, rel(1, last), cols(j)] + yrecv[v].astype(f32)).astype(zs.dtype)

        by_hand = r < nq - DIRECT

        @pl.when(corner & by_hand)
        def _():
            rr(r).start()

        @pl.when(corner & jnp.logical_not(by_hand))
        def _():
            rz(3, r).start()

        @pl.when(corner | jnp.logical_not(by_hand))
        def _():
            rz(2, r).start()
        for slot in range(2):
            @pl.when(has[slot])
            def _():
                rz(slot, r).start()

    def stage_g(r):
        h, j = split(r)

        @pl.when(jnp.logical_not(corner))
        def _():
            rr(r).wait_recv()
            v = (h, rel(2), cols(j))
            zs[v] = (pown[h, 0, rel(2), cols(j)] + yrecv[v].astype(f32) + zr[3, h, :, cols(j)].astype(f32)).astype(zs.dtype)
            rz(2, r).start()

    def stage_s(r):
        h, j = split(r)
        ro(r).wait_recv()
        v = (h, 0, rel(0), cols(j))
        pown[v] += yrecv[h, rel(0), cols(j)].astype(f32)
        for slot in range(4):
            @pl.when(came[slot] & (r >= nq - DIRECT) if slot == 3 else came[slot])
            def _():
                rz(slot, r).wait_recv()
                pown[v] += zr[slot, h, :, cols(j)].astype(f32)
        out_ref[pl.ds(pl.multiple_of(h * hr, hr), hr), cols(j)] = pown[v].astype(out_ref.dtype)

    gather = [(functools.partial(stage_a, s), lag) for s, lag in zip(((0, 1), (2,), (3,)), LAG_A)]
    gather += [(functools.partial(stage_p, k), LAG_P[k]) for k in range(2)]
    start_r = LAG_C + chunks - 1
    reduce_a = [(stage_e, start_r + LAG_E), (stage_f, start_r + LAG_F)]
    late = start_r + max(LAG_F, LAG_G - DIRECT, LAG_S - DEFER)
    early_rows = nq - DEFER

    def run(t, stages):
        for fn, lag in stages:
            @pl.when((t >= lag) & (t < nq + lag))
            def _():
                fn(t - lag)

    def early(t):
        @pl.when(t + AHEAD_Z < nq)
        def _():
            stage0z(t + AHEAD_Z)

        @pl.when(t + AHEAD_Y < nq)
        def _():
            stage0y(t + AHEAD_Y)
        for fn, lag in gather + [(stage_in, LAG_C)]:
            @pl.when(t == TABLE + lag)
            def _():
                fn(None)
        run(t, gather)

    def back(t):
        run(t, reduce_a)

        @pl.when((t >= start_r + LAG_G) & (t < nq - DIRECT + start_r + LAG_G))
        def _():
            stage_g(t - start_r - LAG_G)

        @pl.when((t >= start_r + LAG_S) & (t < early_rows + start_r + LAG_S))
        def _():
            stage_s(t - start_r - LAG_S)

    def first(t, _):
        early(t)
        run(t, [(stage_c, LAG_C)])
        return 0

    def middle(t, _):
        early(t)
        back(t)
        run(t, [(stage_c, LAG_C), (stage_d, start_r)])
        return 0

    def final(t, _):
        back(t)
        run(t, [(stage_d, start_r)])
        return 0

    lax.fori_loop(0, AHEAD_Z, lambda q, _: (stage0z(q), 0)[1], 0)
    lax.fori_loop(0, AHEAD_Y, lambda q, _: (stage0y(q), 0)[1], 0)
    expert_row = lax.broadcasted_iota(jnp.int32, (lanes, rows), 0)
    spread = jnp.zeros((lanes, rows), f32)
    for k in range(ids_ref.shape[0]):
        spread += jnp.where(expert_row == ids_ref[k:k + 1, :], weights_ref[k:k + 1, :].astype(f32), 0.0)
    unit = (lax.broadcasted_iota(jnp.int32, (rows, rows), 0) == lax.broadcasted_iota(jnp.int32, (rows, rows), 1))
    table = lax.dot_general(
        unit.astype(f32).astype(jnp.bfloat16), spread.astype(jnp.bfloat16), (((1,), (1,)), ((), ())),
        preferred_element_type=f32).astype(wg.dtype)
    for h in range(2):
        wg[h, 0, rel(0), :] = table[h * hr:(h + 1) * hr, :]

    stage0z(None)
    stage0y(None)
    for h in range(2):
        own_x[h].wait()
    lax.fori_loop(0, start_r, first, 0)
    lax.fori_loop(start_r, nq + LAG_C, middle, 0)
    lax.fori_loop(nq + LAG_C, nq + late, final, 0)

    def whole(sem, blocks):
        while blocks:
            n = min(blocks, 4 * chunks)
            r = n if n < 4 else n - n % 4
            if n < 4:
                ref = xg.at[0, pl.ds(0, 1), pl.ds(0, hr), pl.ds(0, n * width)]
            else:
                ref = xg.at[0, pl.ds(0, 1), pl.ds(0, col), pl.ds(0, r // 4 * width)]
            sent(sem, ref)
            blocks -= r

    whole(gy_s.at[1, 0], nq)
    whole(gy_s.at[0, 0], nq * last)
    whole(gp_s.at[0], nq * 2 * major)
    for slot in range(4):
        @pl.when((*has, jnp.logical_not(corner))[slot])
        def _():
            whole(gz_s.at[slot, 0], nq)
            sent(gz_s.at[slot, 1], wg.at[:, 0, rel(0), :])
    sent(gy_s.at[1, 1], wg.at[:, 0, rel(0), :])
    sent(gy_s.at[0, 1], wg.at[:, 0, rel(1, last), :])
    sent(gp_s.at[1], wg.at[:, pl.ds(0, 2), :, :])
    whole(rp_s.at[0], nq * 2 * major)
    whole(ry_s.at[0], nq * last)
    lax.fori_loop(early_rows, nq, lambda r, _: (stage_s(r), 0)[1], 0)
    whole(ro_s.at[0], nq)
    for slot in range(4):
        @pl.when((*has, corner)[slot])
        def _():
            whole(rz_s.at[slot], nq)


def fused(tokens, expert_ids, route_weights, w_up, w_down, width=512):
    rows, depth = tokens.shape
    ff = w_up.shape[2]
    experts = lax.axis_size(("node", "local"))
    major = lax.axis_size("local") // 2
    chunks = depth // width
    lanes = -(-experts // LANES) * LANES
    col = major * rows // 2
    bf, f32 = jnp.bfloat16, jnp.float32
    nq = 2 * chunks
    dma = pltpu.SemaphoreType.DMA
    return pl.pallas_call(
        functools.partial(moe_kernel, (rows, major, chunks, width)),
        out_shape=pltpu.VMEM((rows, depth), bf),
        in_specs=[
            pl.BlockSpec(memory_space=pl.ANY),
            pl.BlockSpec(memory_space=pltpu.VMEM),
            pl.BlockSpec(memory_space=pltpu.VMEM),
            pl.BlockSpec(memory_space=pl.ANY),
            pl.BlockSpec(memory_space=pl.ANY),
        ],
        out_specs=pl.BlockSpec(memory_space=pltpu.VMEM),
        scratch_shapes=[
            pltpu.VMEM((2, 4, col, depth), bf),
            pltpu.VMEM((2, 4, col, lanes), bf),
            pltpu.VMEM((depth, ff), bf),
            pltpu.VMEM((ff, depth), bf),
            pltpu.VMEM((4 * col, ff), f32),
            pltpu.VMEM((2, 4 * col, ff), bf),
            pltpu.VMEM((2, 2, col, depth), bf),
            pltpu.VMEM((2, 2, col, depth), bf),
            pltpu.VMEM((2, 2, col, depth), f32),
            pltpu.VMEM((2, col, depth), bf),
            pltpu.VMEM((2, col, depth), bf),
            pltpu.VMEM((2, col, depth), bf),
            pltpu.VMEM((4, 2, rows // 2, depth), bf),
            dma((2,)), dma((chunks,)), dma((chunks,)),
            dma((4, 2)), dma((4, nq + 1)),
            dma((2, 2)), dma((nq + 1,)),
            dma((2,)), dma((nq + 1,)),
            dma((1,)), dma((nq,)),
            dma((1,)), dma((nq,)),
            dma((1,)), dma((nq,)),
            dma((4,)), dma((4, nq)),
        ],
        compiler_params=pltpu.CompilerParams(
            collective_id=0, has_side_effects=True, vmem_limit_bytes=60 * 1024 * 1024),
    )(tokens, expert_ids.T, route_weights.T, w_up, w_down)


def place_rows(targets, groups, width):
    onehot = (targets[:, None] == jnp.arange(groups, dtype=jnp.int32)[None, :]).astype(jnp.int32)
    before = jnp.cumsum(onehot, axis=0) - onehot
    rank = jnp.sum(before * onehot, axis=1)
    return jnp.where(targets >= 0, targets * width + rank, groups * width)


def per_device(tokens, expert_ids, route_weights, w_up, w_down):
    up_matrix = w_up[0]
    down_matrix = w_down[0]
    rows = tokens.shape[0]
    top = expert_ids.shape[1]
    width_d = tokens.shape[1]
    experts = lax.axis_size(("node", "local"))
    most = max(4, 2 * rows * top // experts)
    slot = place_rows(expert_ids.reshape(-1), experts, most)
    source = tokens[jnp.arange(rows * top, dtype=jnp.int32) // top]
    buffer = jnp.zeros((experts * most, width_d), jnp.bfloat16).at[slot].set(source, mode="drop")
    buffer = buffer.reshape(experts, most, width_d)
    received = lax.all_to_all(buffer, ("node", "local"), split_axis=0, concat_axis=0, tiled=True)
    shape = received.shape
    flat = received.reshape(-1, shape[-1])
    hidden = jax.nn.silu(jnp.dot(flat, up_matrix, preferred_element_type=jnp.float32)).astype(
        jnp.bfloat16
    )
    answer = jnp.dot(hidden, down_matrix, preferred_element_type=jnp.float32).astype(jnp.bfloat16)
    done = answer.reshape(shape)
    returned = lax.all_to_all(
        done, ("node", "local"), split_axis=0, concat_axis=0, tiled=True
    ).reshape(experts * most, width_d)
    picked = returned[jnp.minimum(slot, experts * most - 1)].reshape(rows, top, width_d)
    mixed = jnp.einsum("tk,tkd->td", route_weights, picked, preferred_element_type=jnp.float32)
    return mixed.astype(jnp.bfloat16)


def solution(mesh):
    placed = (
        P(("rep", "node", "local"), None),
        P(("rep", "node", "local"), None),
        P(("rep", "node", "local"), None),
        P(("node", "local"), None, None),
        P(("node", "local"), None, None),
    )

    def body(tokens, expert_ids, route_weights, w_up, w_down):
        experts = mesh.shape["node"] * mesh.shape["local"]
        near_dense = experts <= 2 * expert_ids.shape[1]
        if near_dense and mesh.shape["node"] == 2 and mesh.shape["local"] == 8:
            return fused(tokens, expert_ids, route_weights, w_up, w_down)
        return per_device(tokens, expert_ids, route_weights, w_up, w_down)

    return jax.shard_map(
        body,
        mesh=mesh,
        in_specs=placed,
        out_specs=P(("rep", "node", "local"), None),
        check_vma=False,
    )
```

time: 57.9 us -> 54.6 us (0.943)
  Pallas kernels: 57 us -> 53.7 us
    pallas_call x1, Pallas kernels: 57 us -> 53.7 us  [fused(): pl.pallas_call(functools.partial(moe_kernel, (rows, major, chunks, width)...]
where the time goes in v2:
time: 54.6 us; the launch traced here: 54.4 us
  Pallas kernels  53.7 us (98%)
  local copies, waits for them, and re-layouts  0.69 us (1%)
    pallas_call x1, Pallas kernels, fused(): pl.pallas_call(functools.partial(moe_kernel, (rows, major, chunks, width)...  53.7 us

profile of v2, /device:TPU:0, one launch (start us, length us, event | category | flops | bytes accessed | tf_op | source)
XLA Modules:
  0.0 54.4 jit_solution(12160720526164814844)
XLA Ops:
  0.0 53.7 %shard_map.55 = bf16[32,3584]{1,0:T(8,128)(2,1)S(1)} custom-call(bf16[32,3584]{1,0:T(8,128)(2,1)} %x_hbm.1, s32[8,32]{1,0:T(8,128)} %bitcast.2, bf16[8,32]{1,0:T(8,128)(2,1)} %bitcast.3, bf16[1,3584,1024]{2,1,0:T(8,128)(2,1)} %up_hbm.1, bf16[1,1024,3584]{2,1,0:T(8,128)(2,1)} %down_hbm.1), custom_call_target="tpu_custom_call" | custom-call | tf_op jit(solution)/shard_map/pallas_call | solution.py:411
  53.7 0.7 %copy.7 = bf16[32,3584]{1,0:T(8,128)(2,1)} copy(bf16[32,3584]{1,0:T(8,128)(2,1)S(1)} %shard_map.55) | data formatting | bytes 458752

commit v3 on v2

--- a/solution.py
+++ b/solution.py
@@ -9,7 +9,7 @@
 MESH = pl.DeviceIdType.MESH
 LANES = 128
 AHEAD_Z = 2
-AHEAD_Y = 10
+AHEAD_Y = 7
 TABLE = 3
 LAG_A = (1, 1, 3)
 LAG_P = (5, 6)
@@ -18,8 +18,8 @@
 LAG_F = 5
 LAG_G = 8
 LAG_S = 11
-DEFER = 10
-DIRECT = 3
+DEFER = 14
+DIRECT = 2
 
 
 def moe_kernel(sizes, x_hbm, ids_ref, weights_ref, up_hbm, down_hbm, out_ref,
@@ -77,9 +77,6 @@
     def down_copy(j):
         return pltpu.make_async_copy(down_hbm.at[0, :, cols(j)], down.at[:, cols(j)], down_sem.at[j])
 
-    lax.fori_loop(0, chunks, lambda j, _: (up_copy(j).start(), 0)[1], 0)
-    lax.fori_loop(0, chunks, lambda j, _: (down_copy(j).start(), 0)[1], 0)
-
     pl.semaphore_wait(barrier, len(peers))
 
     def split(q):
@@ -329,6 +326,10 @@
             stage_s(t - start_r - LAG_S)
 
     def first(t, _):
+        @pl.when(t < chunks)
+        def _():
+            up_copy(t).start()
+            down_copy(t).start()
         early(t)
         run(t, [(stage_c, LAG_C)])
         return 0

time: 54.6 us -> 53.4 us (0.978)
  Pallas kernels: 53.7 us -> 52.5 us
    pallas_call x1, Pallas kernels: 53.7 us -> 52.5 us  [fused(): pl.pallas_call(functools.partial(moe_kernel, (rows, major, chunks, width)...]
where the time goes in v3:
time: 53.4 us; the launch traced here: 53.2 us
  Pallas kernels  52.5 us (98%)
  local copies, waits for them, and re-layouts  0.69 us (1%)
    pallas_call x1, Pallas kernels, fused(): pl.pallas_call(functools.partial(moe_kernel, (rows, major, chunks, width)...  52.5 us

profile of v3, /device:TPU:0, one launch (start us, length us, event | category | flops | bytes accessed | tf_op | source)
XLA Modules:
  0.0 53.2 jit_solution(9137183340001846302)
XLA Ops:
  0.0 52.5 %shard_map.55 = bf16[32,3584]{1,0:T(8,128)(2,1)S(1)} custom-call(bf16[32,3584]{1,0:T(8,128)(2,1)} %x_hbm.1, s32[8,32]{1,0:T(8,128)} %bitcast.2, bf16[8,32]{1,0:T(8,128)(2,1)} %bitcast.3, bf16[1,3584,1024]{2,1,0:T(8,128)(2,1)} %up_hbm.1, bf16[1,1024,3584]{2,1,0:T(8,128)(2,1)} %down_hbm.1), custom_call_target="tpu_custom_call" | custom-call | tf_op jit(solution)/shard_map/pallas_call | solution.py:412
  52.5 0.7 %copy.7 = bf16[32,3584]{1,0:T(8,128)(2,1)} copy(bf16[32,3584]{1,0:T(8,128)(2,1)S(1)} %shard_map.55) | data formatting | bytes 458752

commit v4 on v3

--- a/solution.py
+++ b/solution.py
@@ -12,7 +12,7 @@
 AHEAD_Y = 7
 TABLE = 3
 LAG_A = (1, 1, 3)
-LAG_P = (5, 6)
+LAG_P = (4, 6)
 LAG_C = 7
 LAG_E = 2
 LAG_F = 5
@@ -24,7 +24,7 @@
 
 def moe_kernel(sizes, x_hbm, ids_ref, weights_ref, up_hbm, down_hbm, out_ref,
                xg, wg, up, down, acc, hid, psend, precv, pown, ysend, yrecv, zs, zr,
-               own_sem, up_sem, down_sem,
+               own_sem, up_sem,
                gz_s, gz_r, gy_s, gy_r, gp_s, gp_r,
                rp_s, rp_r, ry_s, ry_r, ro_s, ro_r, rz_s, rz_r):
     rows, major, chunks, width = sizes
@@ -52,6 +52,7 @@
     came = (z > 0, z < last, z >= 0, corner)
     from_rel = (last, 1, 2, jnp.where(z == 0, last, 1))
     to_rel = (1, last, 2, jnp.where(z == 0, last, 1))
+    lane_of = (0, 0, 1, 2)
     relay_rel = jnp.where(z == 1, last, 1)
 
     barrier = pltpu.get_barrier_semaphore()
@@ -75,7 +76,7 @@
         return pltpu.make_async_copy(up_hbm.at[0, cols(j), :], up.at[cols(j), :], up_sem.at[j])
 
     def down_copy(j):
-        return pltpu.make_async_copy(down_hbm.at[0, :, cols(j)], down.at[:, cols(j)], down_sem.at[j])
+        return pltpu.make_async_copy(down_hbm.at[0, :, cols(j)], down.at[:, cols(j)], up_sem.at[j])
 
     pl.semaphore_wait(barrier, len(peers))
 
@@ -109,15 +110,15 @@
         return x_hbm.at[pl.ds(pl.multiple_of(h * hr, hr), hr), cols(j)], xg.at[h, a, rel(k), cols(j)]
 
     def gz(slot, q):
-        return remote(*own(q, 0, from_rel[slot]), gz_s.at[slot, kind(q)], gz_r.at[slot, idx(q)], nexts[slot])
+        return remote(*own(q, 0, from_rel[slot]), gz_s.at[slot, kind(q)], gz_r.at[lane_of[slot], idx(q)], nexts[slot])
 
     def relay(q):
         return remote(region(q, 0, 1, 2, 1), region(q, 0, 1, relay_rel, 1),
-                      gz_s.at[3, kind(q)], gz_r.at[3, idx(q)], outward)
-
-    def gz_in(slot, q):
-        v = region(q, 0, 1, from_rel[slot], 1)
-        return remote(v, v, gz_s.at[slot, kind(q)], gz_r.at[slot, idx(q)], nexts[2])
+                      gz_s.at[3, kind(q)], gz_r.at[2, idx(q)], outward)
+
+    def gz_in(lane, blocks, q):
+        v = region(q, 0, 1, (1, 2, from_rel[3])[lane], blocks)
+        return remote(v, v, gz_s.at[2, kind(q)], gz_r.at[lane, idx(q)], nexts[2])
 
     def gy(k, q):
         v = own(q, 1, 0) if k is None else (region(q, 0, 1, k, 1), region(q, 1, 1, k, 1))
@@ -144,16 +145,30 @@
     def stage0y(q):
         gy(None, q).start()
 
-    def stage_a(slots, q):
-        for slot in slots:
-            @pl.when(came[slot])
-            def _():
-                gz_in(slot, q).wait_recv()
-                if slot == 2:
-                    @pl.when(jnp.logical_not(corner))
-                    def _():
-                        relay(q).start()
-                gy(from_rel[slot], q).start()
+    def stage_a(lane, q):
+        if lane == 0:
+            @pl.when(corner)
+            def _():
+                gz_in(0, 1, q).wait_recv()
+                gy(jnp.where(z == 0, 1, last), q).start()
+
+            @pl.when(jnp.logical_not(corner))
+            def _():
+                gz_in(0, 2, q).wait_recv()
+                gy(1, q).start()
+                gy(last, q).start()
+        elif lane == 1:
+            gz_in(1, 1, q).wait_recv()
+
+            @pl.when(jnp.logical_not(corner))
+            def _():
+                relay(q).start()
+            gy(2, q).start()
+        else:
+            @pl.when(corner)
+            def _():
+                gz_in(2, 1, q).wait_recv()
+                gy(from_rel[3], q).start()
 
     def stage_p(k, q):
         if k == 1:
@@ -172,7 +187,8 @@
 
         @pl.when(h == 0)
         def _():
-            up_copy(j).wait()
+            both = up.at[pl.ds(0, 2 * width), :]
+            pltpu.make_async_copy(both, both, up_sem.at[j]).wait()
         x = xg[h, :, :, cols(j)].reshape(grp, width)
         part = jnp.dot(x, up[cols(j), :], preferred_element_type=f32)
 
@@ -209,18 +225,15 @@
     def rz(slot, r):
         h, j = split(r)
         return remote(zs.at[h, rel(to_rel[slot]), cols(j)], zr.at[slot, h, :, cols(j)],
-                      rz_s.at[slot], rz_r.at[slot, r], nexts[slot])
+                      rz_s.at[slot], rz_r.at[0, r], nexts[slot])
 
     def rr(r):
         h, j = split(r)
-        return remote(zs.at[h, rel(to_rel[3]), cols(j)], zr.at[3, h, :, cols(j)], rz_s.at[3], rz_r.at[3, r], inward)
+        return remote(zs.at[h, rel(to_rel[3]), cols(j)], zr.at[3, h, :, cols(j)], rz_s.at[3], rz_r.at[1, r], inward)
 
     def stage_d(r):
         h, j = split(r)
 
-        @pl.when(h == 0)
-        def _():
-            down_copy(j).wait()
         part = jnp.dot(hid[h], down[:, cols(j)], preferred_element_type=f32)
         psend[h, :, :, cols(j)] = part[half:, :].astype(psend.dtype).reshape(2, col, width)
         rp(r).start()
@@ -280,14 +293,20 @@
         ro(r).wait_recv()
         v = (h, 0, rel(0), cols(j))
         pown[v] += yrecv[h, rel(0), cols(j)].astype(f32)
+        def arrived(n):
+            blocks = zr.at[pl.ds(0, n), h, :, cols(j)]
+            remote(blocks, blocks, rz_s.at[0], rz_r.at[0, r], nexts[2]).wait_recv()
+
+        two = corner & (r < nq - DIRECT)
+        pl.when(two)(lambda: arrived(2))
+        pl.when(jnp.logical_not(two))(lambda: arrived(3))
         for slot in range(4):
             @pl.when(came[slot] & (r >= nq - DIRECT) if slot == 3 else came[slot])
             def _():
-                rz(slot, r).wait_recv()
                 pown[v] += zr[slot, h, :, cols(j)].astype(f32)
         out_ref[pl.ds(pl.multiple_of(h * hr, hr), hr), cols(j)] = pown[v].astype(out_ref.dtype)
 
-    gather = [(functools.partial(stage_a, s), lag) for s, lag in zip(((0, 1), (2,), (3,)), LAG_A)]
+    gather = [(functools.partial(stage_a, s), lag) for s, lag in zip(range(3), LAG_A)]
     gather += [(functools.partial(stage_p, k), LAG_P[k]) for k in range(2)]
     start_r = LAG_C + chunks - 1
     reduce_a = [(stage_e, start_r + LAG_E), (stage_f, start_r + LAG_F)]
@@ -434,14 +453,14 @@
             pltpu.VMEM((2, col, depth), bf),
             pltpu.VMEM((2, col, depth), bf),
             pltpu.VMEM((4, 2, rows // 2, depth), bf),
-            dma((2,)), dma((chunks,)), dma((chunks,)),
-            dma((4, 2)), dma((4, nq + 1)),
+            dma((2,)), dma((chunks,)),
+            dma((4, 2)), dma((3, nq + 1)),
             dma((2, 2)), dma((nq + 1,)),
             dma((2,)), dma((nq + 1,)),
             dma((1,)), dma((nq,)),
             dma((1,)), dma((nq,)),
             dma((1,)), dma((nq,)),
-            dma((4,)), dma((4, nq)),
+            dma((4,)), dma((2, nq)),
         ],
         compiler_params=pltpu.CompilerParams(
             collective_id=0, has_side_effects=True, vmem_limit_bytes=60 * 1024 * 1024),

time: 53.4 us -> 52.9 us (level)
  no operation moved by 1% of the time
where the time goes in v4:
time: 52.9 us; the launch traced here: 52.7 us
  Pallas kernels  52 us (98%)
  local copies, waits for them, and re-layouts  0.69 us (1%)
    pallas_call x1, Pallas kernels, fused(): pl.pallas_call(functools.partial(moe_kernel, (rows, major, chunks, width)...  52 us

profile of v4, /device:TPU:0, one launch (start us, length us, event | category | flops | bytes accessed | tf_op | source)
XLA Modules:
  0.0 52.7 jit_solution(4277156528009189101)
XLA Ops:
  0.0 52.0 %shard_map.55 = bf16[32,3584]{1,0:T(8,128)(2,1)S(1)} custom-call(bf16[32,3584]{1,0:T(8,128)(2,1)} %x_hbm.1, s32[8,32]{1,0:T(8,128)} %bitcast.2, bf16[8,32]{1,0:T(8,128)(2,1)} %bitcast.3, bf16[1,3584,1024]{2,1,0:T(8,128)(2,1)} %up_hbm.1, bf16[1,1024,3584]{2,1,0:T(8,128)(2,1)} %down_hbm.1), custom_call_target="tpu_custom_call" | custom-call | tf_op jit(solution)/shard_map/pallas_call | solution.py:431
  52.0 0.7 %copy.7 = bf16[32,3584]{1,0:T(8,128)(2,1)} copy(bf16[32,3584]{1,0:T(8,128)(2,1)S(1)} %shard_map.55) | data formatting | bytes 458752

commit v5 on v4

--- a/solution.py
+++ b/solution.py
@@ -8,7 +8,7 @@
 
 MESH = pl.DeviceIdType.MESH
 LANES = 128
-AHEAD_Z = 2
+AHEAD_Z = 3
 AHEAD_Y = 7
 TABLE = 3
 LAG_A = (1, 1, 3)
@@ -136,11 +136,11 @@
         return remote(v, v, gp_s.at[kind(q)], gp_r.at[idx(q)], at_p)
 
     def stage0z(q):
-        gz(2, q).start()
         for d in range(2):
             @pl.when(has[d])
             def _():
                 gz(d, q).start()
+        gz(2, q).start()
 
     def stage0y(q):
         gy(None, q).start()
@@ -334,11 +334,10 @@
         run(t, gather)
 
     def back(t):
+        @pl.when((t >= start_r + LAG_G) & (t < nq - DIRECT + start_r + LAG_G))
+        def _():
+            stage_g(t - start_r - LAG_G)
         run(t, reduce_a)
-
-        @pl.when((t >= start_r + LAG_G) & (t < nq - DIRECT + start_r + LAG_G))
-        def _():
-            stage_g(t - start_r - LAG_G)
 
         @pl.when((t >= start_r + LAG_S) & (t < early_rows + start_r + LAG_S))
         def _():

time: 52.9 us -> 53 us (level)
  no operation moved by 1% of the time
where the time goes in v5:
time: 53 us; the launch traced here: 52.8 us
  Pallas kernels  52.1 us (98%)
  local copies, waits for them, and re-layouts  0.69 us (1%)
    pallas_call x1, Pallas kernels, fused(): pl.pallas_call(functools.partial(moe_kernel, (rows, major, chunks, width)...  52.1 us

profile of v5, /device:TPU:0, one launch (start us, length us, event | category | flops | bytes accessed | tf_op | source)
XLA Modules:
  0.0 52.8 jit_solution(7237806478698448245)
XLA Ops:
  0.0 52.1 %shard_map.55 = bf16[32,3584]{1,0:T(8,128)(2,1)S(1)} custom-call(bf16[32,3584]{1,0:T(8,128)(2,1)} %x_hbm.1, s32[8,32]{1,0:T(8,128)} %bitcast.2, bf16[8,32]{1,0:T(8,128)(2,1)} %bitcast.3, bf16[1,3584,1024]{2,1,0:T(8,128)(2,1)} %up_hbm.1, bf16[1,1024,3584]{2,1,0:T(8,128)(2,1)} %down_hbm.1), custom_call_target="tpu_custom_call" | custom-call | tf_op jit(solution)/shard_map/pallas_call | solution.py:430
  52.1 0.7 %copy.7 = bf16[32,3584]{1,0:T(8,128)(2,1)} copy(bf16[32,3584]{1,0:T(8,128)(2,1)S(1)} %shard_map.55) | data formatting | bytes 458752
